TPU v7x, 512 devices: a whole 4x8x8 slice. The times are simulated.
512 devices in a mesh: occ: 128 (over z_lo, x, y), grp: 4 (over z_hi, core).
Axes of the slice: x: 4, y: 8, z: 8 (z_hi: 2, z_lo: 4; z = z_hi * 4 + z_lo), core: 2. Of those that a mesh axis runs over, the one named last changes fastest.
Arguments:
- slabs: float32 [512, 512, 1024], P(('occ', 'grp')), may hold values from -4 to 4
- occ_energy: float32 [512], replicated, may hold values from -1.5 to -0.3
- vir_energy: float32 [512], replicated, may hold values from 0.1 to 3
- pair_mask: int32 [512, 2], replicated, may hold values from 0 to 1, as said below
Outputs:
- aux_grad: float32 [512, 512, 1024], P(('occ', 'grp'))
- vir_density: float32 [512, 512], P('occ')
Inputs may be any that keep to these rules, and one draw needn't show every extreme that they name: Entries are 0 or 1; orbital 0 is paired with all of its 2 partners, and so is every orbital i >= 512 - 1 - 2 (pair_mask[i, k - 1] = 1 for every 1 <= k <= 2 on those rows).
All inputs are finite; a program needn't handle non-finite values.
Results may differ from a plain program's by a relative error of at most 0.0003.
Values sent between devices are 32-bit elements; how exact they have to be, the bound alone decides.
A program may use at most 128 MiB of HBM per device.

v0:
```python
import jax
import jax.numpy as jnp
from jax import lax
from jax.sharding import PartitionSpec as P

highest = lax.Precision.HIGHEST


def shifted(block, axis, distance):
    devices = range(lax.axis_size(axis))
    route = [(i - distance, i) for i in devices if i - distance in devices]
    return lax.ppermute(block, axis, route)


def pair_terms(left_slab, right_slab, left_energy, right_energy, virtual):
    coulomb = jnp.dot(
        left_slab, right_slab.T, precision=highest, preferred_element_type=jnp.float32
    )
    denominator = left_energy + right_energy - virtual[:, None] - virtual[None, :]
    amplitude = coulomb / denominator
    grad_left = jnp.dot(
        amplitude, right_slab, precision=highest, preferred_element_type=jnp.float32
    )
    grad_right = jnp.dot(
        amplitude.T, left_slab, precision=highest, preferred_element_type=jnp.float32
    )
    density = jnp.dot(amplitude, amplitude.T, precision=highest, preferred_element_type=jnp.float32)
    density = density + jnp.dot(
        amplitude.T, amplitude, precision=highest, preferred_element_type=jnp.float32
    )
    return (grad_left, grad_right, density)


def body(slabs, occ_energy, vir_energy, pair_mask):
    own_slab = slabs[0]
    orbitals = lax.axis_size(("occ", "grp"))
    position = lax.axis_index(("occ", "grp"))
    own_energy = lax.dynamic_index_in_dim(occ_energy, position, 0, keepdims=False)
    grad_left, grad_right, density = pair_terms(
        own_slab, own_slab, own_energy, own_energy, vir_energy
    )
    gradient = grad_left + grad_right
    offsets = pair_mask.shape[1]
    for offset in range(1, offsets + 1):
        column = pair_mask[:, offset - 1]
        partner_index = jnp.minimum(position + offset, orbitals - 1)
        partner_energy = lax.dynamic_index_in_dim(occ_energy, partner_index, 0, keepdims=False)
        forward_flag = lax.dynamic_index_in_dim(column, position, 0, keepdims=False)
        forward_active = (forward_flag == 1) & (position + offset < orbitals)
        partner_slab = shifted(own_slab, ("occ", "grp"), -offset)

        def whole_pair():
            return pair_terms(own_slab, partner_slab, own_energy, partner_energy, vir_energy)

        def empty_pair():
            return (jnp.zeros_like(own_slab), jnp.zeros_like(own_slab), jnp.zeros_like(density))

        grad_left, grad_right, term = lax.cond(forward_active, whole_pair, empty_pair)
        returned = shifted(grad_right, ("occ", "grp"), offset)
        gradient = gradient + grad_left + returned
        density = density + term
    row_count = density.shape[0] // lax.axis_size("occ")
    summed = lax.psum(density, ("occ", "grp"))
    own_rows = lax.dynamic_slice_in_dim(summed, lax.axis_index("occ") * row_count, row_count, 0)
    return (gradient[None], own_rows / orbitals)


def solution(mesh):
    placed = (P(("occ", "grp"), None, None), P(), P(), P())
    return jax.shard_map(
        body,
        mesh=mesh,
        in_specs=placed,
        out_specs=(P(("occ", "grp"), None, None), P("occ", None)),
        check_vma=False,
    )
```

profile of v0, /device:TPU:24, one launch (start us, length us, event | category | flops | bytes accessed | tf_op | source)
XLA Modules:
  0.0 632.4 jit_solution(11234347557603762785)
XLA Ops:
  7.2 0.0 all-reduce.2.cloned.1.call-start
  7.2 10.2 %collective-permute-start = (f32[512,1024]{1,0:T(8,128)}, f32[512,1024]{1,0:T(8,128)S(1)}, u32[]{:S(2)}, u32[]{:S(2)}) collective-permute-start(f32[512,1024]{1,0:T(8,128)} %bitcast.34), channel_id=1, source_target_pairs={{1,0},{2,1},{3,2},{4,3},{5,4},{6,5},{7,6},{8,7},{9,8},{10,9},{11,1... | collective-permute-start | bytes 6291464 | tf_op jit(solution)/shard_map/ppermute | solution.py:12
  17.5 2.5 collective-permute-start.2
  20.0 1.3 dynamic_slice.24
  21.2 0.8 fusion.27
  22.0 0.6 fusion.28
  25.2 72.1 %collective-permute-done = f32[512,1024]{1,0:T(8,128)S(1)} collective-permute-done((f32[512,1024]{1,0:T(8,128)}, f32[512,1024]{1,0:T(8,128)S(1)}, u32[]{:S(2)}, u32[]{:S(2)}) %collective-permute-start) | collective-permute-done | bytes 2097184 | tf_op jit(solution)/shard_map/ppermute | solution.py:12
  97.2 2.2 conditional.2
  97.2 0.2 broadcast.20
  97.5 1.6 broadcast.20.clone
  99.1 0.1 broadcast.21
  99.4 4.8 collective-permute-start.1
  104.3 134.5 %collective-permute-done.2 = f32[512,1024]{1,0:T(8,128)} collective-permute-done((f32[512,1024]{1,0:T(8,128)}, f32[512,1024]{1,0:T(8,128)}, u32[]{:S(2)}, u32[]{:S(2)}) %collective-permute-start.2) | collective-permute-done | bytes 2097184 | tf_op jit(solution)/shard_map/ppermute | solution.py:12
  238.8 4.5 conditional.3
  238.8 1.6 broadcast.22
  240.4 1.6 broadcast.22.clone
  242.0 1.1 broadcast.23
  243.3 0.0 copy-start.8
  243.3 1.9 collective-permute-start.3
  245.2 0.7 broadcast_subtract_fusion.2
  245.9 5.7 fusion.25
  251.7 2.3 fusion
  254.0 2.2 fusion.12
  256.2 0.0 copy-start
  256.2 2.7 add_add_fusion
  258.9 0.0 all-reduce.2.cloned.1.call-update
  259.0 6.3 fusion.4
  265.3 5.2 fusion.6
  270.5 345.6 %all-reduce.2.cloned.1.call-done = f32[512,512]{1,0:T(8,128)} async-done(((f32[512,512]{1,0:T(8,128)}), f32[512,512]{1,0:T(8,128)}) %all-reduce.2.cloned.1.call-update) | async-done | bytes 1048592 | tf_op jit(solution)/shard_map/psum | solution.py:63
  616.1 1.3 dynamic-slice_multiply_fusion
  617.4 0.0 collective-permute-done.1
  617.4 7.7 %add_bitcast_fusion = f32[1,512,1024]{2,1,0:T(8,128)} fusion(f32[512,1024]{1,0:T(8,128)} %collective-permute-done.3, f32[512,1024]{1,0:T(8,128)} %get-tuple-element.104, f32[512,1024]{1,0:T(8,128)} %collective-permute-done.1, f32[512,1024]{1,0:T(8,128)} %copy-done.3, f32[512,1024]{1,0:T(8,128)} %fusion.6, f32[512,1024]{1,0:T(8,128)} %fusion.4), kind=kLoop, calls=%fused_computation.6 | loop fusion | flops 2621440 | bytes 14680064 | tf_op jit(solution)/shard_map/broadcast_in_dim | solution.py:65
  (9 shorter events, 0.0 us)
Async XLA Ops:
  7.2 608.9 %all-reduce.2.cloned.1.call-start = ((), (), s32[]{:S(2)}) async-start(), calls=%async_computation | async-start | bytes 2097152 | tf_op jit(solution)/shard_map/psum | solution.py:63
  7.2 90.0 %collective-permute-start = (f32[512,1024]{1,0:T(8,128)}, f32[512,1024]{1,0:T(8,128)S(1)}, u32[]{:S(2)}, u32[]{:S(2)}) collective-permute-start(f32[512,1024]{1,0:T(8,128)} %bitcast.34), channel_id=1, source_target_pairs={{1,0},{2,1},{3,2},{4,3},{5,4},{6,5},{7,6},{8,7},{9,8},{10,9},{11,1... | collective-permute-start | bytes 6291464 | tf_op jit(solution)/shard_map/ppermute | solution.py:12
  17.5 221.3 %collective-permute-start.2 = (f32[512,1024]{1,0:T(8,128)}, f32[512,1024]{1,0:T(8,128)}, u32[]{:S(2)}, u32[]{:S(2)}) collective-permute-start(f32[512,1024]{1,0:T(8,128)} %bitcast.35), channel_id=1, source_target_pairs={{2,0},{3,1},{4,2},{5,3},{6,4},{7,5},{8,6},{9,7},{10,8},{11,9},{12,... | collective-permute-start | bytes 6291464 | tf_op jit(solution)/shard_map/ppermute | solution.py:12
  99.4 139.4 %copy-start.3 = (f32[512,1024]{1,0:T(8,128)}, f32[512,1024]{1,0:T(8,128)S(1)}, u32[]{:S(2)}) copy-start(f32[512,1024]{1,0:T(8,128)S(1)} %get-tuple-element.102) | copy-start | bytes 6291460
  99.4 518.0 %collective-permute-start.1 = (f32[512,1024]{1,0:T(8,128)}, f32[512,1024]{1,0:T(8,128)}, u32[]{:S(2)}, u32[]{:S(2)}) collective-permute-start(f32[512,1024]{1,0:T(8,128)} %get-tuple-element.103), channel_id=1, source_target_pairs={{0,1},{1,2},{2,3},{3,4},{4,5},{5,6},{6,7},{7,8},{8,9},{9,10},{10,1... | collective-permute-start | bytes 6291464 | tf_op jit(solution)/shard_map/ppermute | solution.py:12
  243.3 8.4 %copy-start.8 = (f32[512]{0:T(512)S(1)}, f32[512]{0:T(512)}, u32[]{:S(2)}) copy-start(f32[512]{0:T(512)} %param.10) | copy-start | bytes 6148
  243.3 374.1 %collective-permute-start.3 = (f32[512,1024]{1,0:T(8,128)}, f32[512,1024]{1,0:T(8,128)}, u32[]{:S(2)}, u32[]{:S(2)}) collective-permute-start(f32[512,1024]{1,0:T(8,128)} %get-tuple-element.105), channel_id=1, source_target_pairs={{0,2},{1,3},{2,4},{3,5},{4,6},{5,7},{6,8},{7,9},{8,10},{9,11},{10,... | collective-permute-start | bytes 6291464 | tf_op jit(solution)/shard_map/ppermute | solution.py:12
  251.7 2.3 copy-start.4
  256.2 2.8 copy-start
  259.0 6.3 copy-start.5
Sparse Core Ops, SparseCore 0:
  259.1 356.9 all-reduce.1
where the time goes:
time: 643 us; the launch traced here: 632 us
  waiting for transfers between devices  552 us (86%)
  matrix products  21.8 us (3%)
  starting transfers between devices  19.5 us (3%)
  between operations  17.2 us (3%)
  other arithmetic  13 us (2%)
  local copies, waits for them, and re-layouts  8.33 us (1%)
    psum x1, waiting for transfers between devices, body(): summed = lax.psum(density, ('occ', 'grp'))  346 us
    ppermute x4, waiting for transfers between devices, shifted(): return lax.ppermute(block, axis, route)  207 us
    ppermute x4, starting transfers between devices, shifted(): return lax.ppermute(block, axis, route)  19.5 us
  transfers between devices with their start and end apart: 5, of which 3 were waited for; matrix products, arithmetic and copies ran while one was open for 6% of the time, Pallas kernels for 0%

commit v1 on v0

--- a/solution.py
+++ b/solution.py
@@ -60,7 +60,7 @@
         gradient = gradient + grad_left + returned
         density = density + term
     row_count = density.shape[0] // lax.axis_size("occ")
-    summed = lax.psum(density, ("occ", "grp"))
+    summed = lax.psum(lax.psum(density, "occ"), "grp")
     own_rows = lax.dynamic_slice_in_dim(summed, lax.axis_index("occ") * row_count, row_count, 0)
     return (gradient[None], own_rows / orbitals)
 

time: 643 us -> 1810 us (2.81)
  the two profiles are of different devices: /device:TPU:24 before, /device:TPU:1 now
where the time goes in v1:
time: 1810 us; the launch traced here: 1800 us
  waiting for transfers between devices  1650 us (91%)
  starting transfers between devices  62.4 us (3%)
  matrix products  42.3 us (2%)
    psum x2, waiting for transfers between devices, body(): summed = lax.psum(lax.psum(density, 'occ'), 'grp')  1590 us
    ppermute x4, starting transfers between devices, shifted(): return lax.ppermute(block, axis, route)  62.3 us
    ppermute x4, waiting for transfers between devices, shifted(): return lax.ppermute(block, axis, route)  58.7 us
  transfers between devices with their start and end apart: 6, of which 4 were waited for; matrix products, arithmetic and copies ran while one was open for 2% of the time, Pallas kernels for 0%

profile of v1, /device:TPU:1, one launch (start us, length us, event | category | flops | bytes accessed | tf_op | source)
XLA Modules:
  0.0 1804.8 jit_solution(5705024909884368826)
XLA Ops:
  7.2 8.8 collective-permute-start
  16.0 1.3 collective-permute-start.2
  17.3 1.3 dynamic_slice.24
  18.6 0.8 fusion.27
  19.4 0.6 fusion.28
  22.5 0.7 broadcast_subtract_fusion.2
  23.2 5.7 fusion.25
  29.0 2.3 fusion
  31.3 3.2 fusion.12
  34.5 58.2 %collective-permute-done = f32[512,1024]{1,0:T(8,128)} collective-permute-done((f32[512,1024]{1,0:T(8,128)}, f32[512,1024]{1,0:T(8,128)}, u32[]{:S(2)}, u32[]{:S(2)}) %collective-permute-start) | collective-permute-done | bytes 2097184 | tf_op jit(solution)/shard_map/ppermute | solution.py:12
  92.7 13.7 conditional.2
  92.7 1.6 broadcast.20
  94.4 1.6 broadcast.20.clone
  95.9 0.1 broadcast.21
  106.4 0.5 collective-permute-done.2
  106.9 23.2 %conditional.3 = (f32[512,1024]{1,0:T(8,128)}, f32[512,1024]{1,0:T(8,128)}, f32[512,512]{1,0:T(8,128)}) conditional(s32[]{:T(128)} %convert_element_type.7, () %tuple.32, (f32[512,1024]{1,0:T(8,128)S(1)}, f32[512,1024]{1,0:T(8,128)}, s32[]{:T(128)}, f32[512]{0:T(512)S(1)}, f32[]{:T(128)}, /*index=5*/f32[512]{0:T(512)S(1)}) %tuple.50), branch_computations={%region_2.3_spmd, %region_3.4_spmd} | conditional | flops 12885688320 | bytes 20979810 | solution.py:58
  106.9 0.6 dynamic_slice.19
  108.7 5.1 convolution_divide_fusion.1
  113.9 1.9 fusion.35
  115.8 2.9 convolution_add_fusion.1
  118.7 6.5 fusion.33
  125.1 4.8 fusion.34
  130.1 2.9 add_add_fusion
  133.1 0.0 all-reduce.5.cloned.1.call-start
  133.1 49.7 %collective-permute-start.1 = (f32[512,1024]{1,0:T(8,128)}, f32[512,1024]{1,0:T(8,128)}, u32[]{:S(2)}, u32[]{:S(2)}) collective-permute-start(f32[512,1024]{1,0:T(8,128)} %get-tuple-element.103), channel_id=1, source_target_pairs={{0,1},{1,2},{2,3},{3,4},{4,5},{5,6},{6,7},{7,8},{8,9},{9,10},{10,1... | collective-permute-start | bytes 6291464 | tf_op jit(solution)/shard_map/ppermute | solution.py:12
  182.8 2.6 collective-permute-start.3
  185.4 1437.9 %all-reduce.3.cloned.1.call-done = f32[512,512]{1,0:T(8,128)} async-done(((f32[512,512]{1,0:T(8,128)}), f32[512,512]{1,0:T(8,128)}) %all-reduce.3.cloned.1.call-update) | async-done | bytes 1048592 | tf_op jit(solution)/shard_map/psum | solution.py:63
  1623.4 5.0 fusion.4
  1628.3 4.9 fusion.6
  1633.3 155.5 %all-reduce.5.cloned.1.call-done = f32[512,512]{1,0:T(8,128)} async-done(((f32[512,512]{1,0:T(8,128)}), f32[512,512]{1,0:T(8,128)}) %all-reduce.5.cloned.1.call-update) | async-done | bytes 1048592 | tf_op jit(solution)/shard_map/psum | solution.py:63
  1788.7 1.3 dynamic-slice_multiply_fusion
  1790.0 7.7 add_bitcast_fusion
  (16 shorter events, 0.1 us)
Async XLA Ops:
  7.2 21.8 %copy-start.3 = (f32[512]{0:T(512)S(1)}, f32[512]{0:T(512)}, u32[]{:S(2)}) copy-start(f32[512]{0:T(512)} %param.10) | copy-start | bytes 6148
  7.2 1616.2 %all-reduce.3.cloned.1.call-start = ((), (), s32[]{:S(2)}) async-start(), calls=%async_computation | async-start | bytes 2097152 | tf_op jit(solution)/shard_map/psum | solution.py:63
  7.2 85.5 %collective-permute-start = (f32[512,1024]{1,0:T(8,128)}, f32[512,1024]{1,0:T(8,128)}, u32[]{:S(2)}, u32[]{:S(2)}) collective-permute-start(f32[512,1024]{1,0:T(8,128)} %bitcast.34), channel_id=1, source_target_pairs={{1,0},{2,1},{3,2},{4,3},{5,4},{6,5},{7,6},{8,7},{9,8},{10,9},{11,1... | collective-permute-start | bytes 6291464 | tf_op jit(solution)/shard_map/ppermute | solution.py:12
  16.0 90.9 %collective-permute-start.2 = (f32[512,1024]{1,0:T(8,128)}, f32[512,1024]{1,0:T(8,128)}, u32[]{:S(2)}, u32[]{:S(2)}) collective-permute-start(f32[512,1024]{1,0:T(8,128)} %bitcast.35), channel_id=1, source_target_pairs={{2,0},{3,1},{4,2},{5,3},{6,4},{7,5},{8,6},{9,7},{10,8},{11,9},{12,... | collective-permute-start | bytes 6291464 | tf_op jit(solution)/shard_map/ppermute | solution.py:12
  29.0 2.3 copy-start.1
  31.3 61.4 %copy-start = (f32[1,512,1024]{2,1,0:T(8,128)S(1)}, f32[1,512,1024]{2,1,0:T(8,128)}, u32[]{:S(2)}) copy-start(f32[1,512,1024]{2,1,0:T(8,128)} %param.8) | copy-start | bytes 6291460
  31.3 61.4 %copy-start.4 = (f32[512]{0:T(512)S(1)}, f32[512]{0:T(512)}, u32[]{:S(2)}) copy-start(f32[512]{0:T(512)} %param.9) | copy-start | bytes 6148
  133.0 1490.3 %copy-start.2 = (f32[512,512]{1,0:T(8,128)S(1)}, f32[512,512]{1,0:T(8,128)}, u32[]{:S(2)}) copy-start(f32[512,512]{1,0:T(8,128)} %copy-done.1) | copy-start | bytes 3145732
  133.1 1655.7 %all-reduce.5.cloned.1.call-start = ((), (), s32[]{:S(2)}) async-start(), calls=%async_computation.1 | async-start | bytes 2097152 | tf_op jit(solution)/shard_map/psum | solution.py:63
  133.1 1656.9 %collective-permute-start.1 = (f32[512,1024]{1,0:T(8,128)}, f32[512,1024]{1,0:T(8,128)}, u32[]{:S(2)}, u32[]{:S(2)}) collective-permute-start(f32[512,1024]{1,0:T(8,128)} %get-tuple-element.103), channel_id=1, source_target_pairs={{0,1},{1,2},{2,3},{3,4},{4,5},{5,6},{6,7},{7,8},{8,9},{9,10},{10,1... | collective-permute-start | bytes 6291464 | tf_op jit(solution)/shard_map/ppermute | solution.py:12
  182.8 1607.3 %collective-permute-start.3 = (f32[512,1024]{1,0:T(8,128)}, f32[512,1024]{1,0:T(8,128)}, u32[]{:S(2)}, u32[]{:S(2)}) collective-permute-start(f32[512,1024]{1,0:T(8,128)} %get-tuple-element.105), channel_id=1, source_target_pairs={{0,2},{1,3},{2,4},{3,5},{4,6},{5,7},{6,8},{7,9},{8,10},{9,11},{10,... | collective-permute-start | bytes 6291464 | tf_op jit(solution)/shard_map/ppermute | solution.py:12
Sparse Core Ops, SparseCore 0:
  133.2 1490.1 all-reduce.2
  1626.3 162.3 all-reduce.4
